TPU v7x, 256 devices: a whole 4x4x8 slice. The times are simulated.
256 devices in a mesh: section: 4 (over y), seq: 64 (over z, x, core).
Axes of the slice: x: 4, y: 4, z: 8, core: 2. Of those that a mesh axis runs over, the one named last changes fastest.
Arguments:
- span_inputs: bfloat16 [4, 2048, 3, 8192], P('section', 'seq'), may hold values from -28 to 28
- out_grad: bfloat16 [4, 2048, 8192], P('section', 'seq'), may hold values from -48 to 48
- past_cache: bfloat16 [4, 3072, 2, 64, 128], P('section', None, None, 'seq'), may hold values from -5 to 5
- past_accum: float32 [4, 3072, 2, 64, 128], P('section', None, None, 'seq'), may hold values from -0.6 to 0.6
- offsets: int32 [4], P('section'), may hold values from 0 to 3072, as said below
- lengths: int32 [4], P('section'), may hold values from 1024 to 2048, as said below
Outputs:
- next_grads: bfloat16 [4, 2048, 3, 8192], P('section', 'seq')
- new_accum: float32 [4, 3072, 2, 64, 128], P('section', None, None, 'seq')
Inputs may be any that keep to these rules, and one draw needn't show every extreme that they name: The first offsets[s] rows of past_cache[s] and past_accum[s] belong to the sequence; one section's offset is 3072. Rows of a span from lengths[s] on are padding; one section's length is 2048.
All inputs are finite; a program needn't handle non-finite values.
Results may differ from a plain program's by a relative error of at most 0.0068.
Values may be sent and summed in bfloat16 or wider, within the bound.
No kernel may reach another device: no remote copies, remote signals or barrier semaphores. Data moves between devices by JAX's collectives and lax.ppermute only.
A program may use at most 128 MiB of HBM per device.

v0:
```python
import math
import jax
import jax.numpy as jnp
from jax import lax
from jax.sharding import PartitionSpec as P

HEADS = 64
DH = 128


def from_behind(block, axis, distance):
    devices = range(lax.axis_size(axis))
    route = [((i - distance) % len(devices), i) for i in devices]
    return lax.ppermute(block, axis, route)


def per_device(span_inputs, out_grad, past_cache, past_accum, offsets, lengths):
    scale_factor = 1.0 / math.sqrt(DH)
    tok_rows = span_inputs.shape[1]
    local_rows = span_inputs[0].reshape(tok_rows, 3, HEADS, DH)
    upstream = out_grad[0].reshape(tok_rows, 1, HEADS, DH)
    offset = offsets[0]
    length = lengths[0]
    cached = past_cache[0]
    past_len = cached.shape[0]
    head_inputs, head_dout = (
        lax.all_to_all(local_rows, "seq", split_axis=2, concat_axis=0, tiled=True),
        lax.all_to_all(upstream, "seq", split_axis=2, concat_axis=0, tiled=True),
    )
    span_len = head_inputs.shape[0]
    local_heads = head_inputs.shape[2]
    block_rows = min(512, span_len)
    block_count = span_len // block_rows
    all_keys = jnp.concatenate([cached[:, 0], head_inputs[:, 1]], axis=0)
    all_values = jnp.concatenate([cached[:, 1], head_inputs[:, 2]], axis=0)
    key_count = all_keys.shape[0]
    queries = head_inputs[:, 0].reshape(block_count, block_rows, local_heads, DH)
    starts = jnp.arange(block_count, dtype=jnp.int32) * block_rows
    key_index = jnp.arange(key_count, dtype=jnp.int32)
    in_span = key_index - past_len

    def scores(query_block, start):
        query_pos = start + jnp.arange(block_rows, dtype=jnp.int32)
        visible = jnp.where(
            key_index[None, :] < past_len,
            key_index[None, :] < offset,
            (in_span[None, :] <= query_pos[:, None]) & (in_span[None, :] < length),
        )
        raw_scores = (
            jnp.einsum("qhd,khd->hqk", query_block, all_keys, preferred_element_type=jnp.float32)
            * scale_factor
        )
        return jnp.where(visible[None], raw_scores, -jnp.inf)

    def backward_block(running, query_block, dout_block, masked):
        grad_keys, grad_values = running
        row_max = jnp.max(masked, axis=-1, keepdims=True)
        exp_terms = jnp.exp(masked - row_max)
        attention = exp_terms / jnp.sum(exp_terms, axis=-1, keepdims=True)
        attention_low = attention.astype(jnp.bfloat16)
        dprobs = jnp.einsum(
            "qhd,khd->hqk", dout_block, all_values, preferred_element_type=jnp.float32
        )
        row_delta = jnp.sum(attention * dprobs, axis=-1, keepdims=True)
        dscores = (attention * (dprobs - row_delta)).astype(jnp.bfloat16)
        grad_query = (
            jnp.einsum("hqk,khd->qhd", dscores, all_keys, preferred_element_type=jnp.float32)
            * scale_factor
        ).astype(jnp.bfloat16)
        grad_keys = (
            grad_keys
            + jnp.einsum("hqk,qhd->khd", dscores, query_block, preferred_element_type=jnp.float32)
            * scale_factor
        )
        grad_values = grad_values + jnp.einsum(
            "hqk,qhd->khd", attention_low, dout_block, preferred_element_type=jnp.float32
        )
        return ((grad_keys, grad_values), grad_query)

    zero_grads = (
        jnp.zeros((key_count, local_heads, DH), jnp.float32),
        jnp.zeros((key_count, local_heads, DH), jnp.float32),
    )
    rows_index = jnp.arange(span_len, dtype=jnp.int32)
    cleared = jnp.where(
        (rows_index < length)[:, None, None], head_dout[:, 0], jnp.zeros((), jnp.bfloat16)
    )
    dout_blocks = cleared.reshape(block_count, block_rows, local_heads, DH)

    def scan_step(running, scan_items):
        query_block, dout_block, start = scan_items
        return backward_block(running, query_block, dout_block, scores(query_block, start))

    (grad_keys, grad_values), grad_query = lax.scan(
        scan_step, zero_grads, (queries, dout_blocks, starts)
    )
    new_accum = past_accum[0] + jnp.stack([grad_keys[:past_len], grad_values[:past_len]], axis=1)
    span_grads = jnp.stack(
        [
            grad_query.reshape(span_len, local_heads, DH),
            grad_keys[past_len:].astype(jnp.bfloat16),
            grad_values[past_len:].astype(jnp.bfloat16),
        ],
        axis=1,
    )
    regrouped = lax.all_to_all(span_grads, "seq", split_axis=0, concat_axis=2, tiled=True)
    moved = from_behind(regrouped, "section", -1)
    return (moved.reshape(1, tok_rows, 3, HEADS * DH), new_accum[None])


def solution(mesh):
    in_specs = (
        P("section", "seq", None, None),
        P("section", "seq", None),
        P("section", None, None, "seq", None),
        P("section", None, None, "seq", None),
        P("section"),
        P("section"),
    )
    out_specs = (P("section", "seq", None, None), P("section", None, None, "seq", None))
    return jax.shard_map(
        per_device, mesh=mesh, in_specs=in_specs, out_specs=out_specs, check_vma=False
    )
```

profile of v0, /device:TPU:56, one launch (start us, length us, event | category | flops | bytes accessed | tf_op | source)
XLA Modules:
  0.0 327.7 jit_solution(9047187464734884413)
XLA Ops:
  3.1 11.6 %all-to-all-start.1 = ((bf16[32,1,64,128]{3,0,1,2:T(8,128)(2,1)}), bf16[32,1,64,128]{3,0,1,2:T(8,128)(2,1)S(1)}, u32[]{:S(2)}, u32[]{:S(2)}) async-start(bf16[32,1,64,128]{3,0,1,2:T(8,128)(2,1)} %copy.52), calls=%async_computation.1 | async-start | bytes 1048576 | tf_op jit(solution)/shard_map/all_to_all | solution.py:28
  15.1 2.2 copy.49
  17.3 14.1 %all-to-all-done.1 = bf16[32,1,64,128]{3,0,1,2:T(8,128)(2,1)S(1)} async-done(((bf16[32,1,64,128]{3,0,1,2:T(8,128)(2,1)}), bf16[32,1,64,128]{3,0,1,2:T(8,128)(2,1)S(1)}, u32[]{:S(2)}, u32[]{:S(2)}) %all-to-all-start.1) | async-done | bytes 524320 | tf_op jit(solution)/shard_map/all_to_all | solution.py:28
  32.2 6.9 %all-to-all-start = ((bf16[32,3,64,128]{3,0,1,2:T(8,128)(2,1)}), bf16[32,3,64,128]{3,0,1,2:T(8,128)(2,1)}, u32[]{:S(2)}, u32[]{:S(2)}) async-start(bf16[32,3,64,128]{3,0,1,2:T(8,128)(2,1)} %copy.49), calls=%async_computation | async-start | bytes 3145728 | tf_op jit(solution)/shard_map/all_to_all | solution.py:27
  39.1 2.7 copy.66
  43.4 2.4 slice_bitcast_fusion
  45.7 2.2 select_bitcast_fusion
  47.9 30.2 %all-to-all-done = bf16[32,3,64,128]{3,0,1,2:T(8,128)(2,1)} async-done(((bf16[32,3,64,128]{3,0,1,2:T(8,128)(2,1)}), bf16[32,3,64,128]{3,0,1,2:T(8,128)(2,1)}, u32[]{:S(2)}, u32[]{:S(2)}) %all-to-all-start) | async-done | bytes 1572896 | tf_op jit(solution)/shard_map/all_to_all | solution.py:27
  78.1 1.8 copy.50
  80.8 1.7 pad_maximum_fusion.1
  82.5 130.7 %while.16 = (s32[]{:T(128)}, f32[5120,1,128]{0,2,1:T(8,128)S(1)}, f32[5120,1,128]{0,2,1:T(8,128)}, bf16[4,512,1,128]{3,1,2,0:T(8,128)(2,1)}, bf16[4,512,1,128]{3...) while((s32[]{:T(128)}, f32[5120,1,128]{0,2,1:T(8,128)S(1)}, ...), condition=%wide.region_4.5_spmd.clone.clone, body=%wide.region_0.4_spmd.clone.clone.sunk | while | flops 3411304448 | bytes 200771376 | solution.py:94
  85.1 4.6 %fusion.62 = (f32[512]{0:T(512)S(1)}, f32[512,5120]{1,0:T(8,128)S(1)}) fusion(bf16[5120,1,128]{2,0,1:T(8,128)(2,1)} %get-tuple-element.356, bf16[4,512,1,128]{3,1,2,0:T(8,128)(2,1)} %get-tuple-element.352, s32[]{:T(128)} %get-tuple-element.335, pred[5120]{0:T(1024)(128)(4,1)S(1)} %get-tuple-element.316, s32[512]{0:T(512)S(1)} %iota_add_fusion.4, ...), kind=kOutput, calls=%fused_computation.57.clone.1 | convolution fusion | flops 686816768 | bytes 11968000 | tf_op jit(solution)/shard_map/while/body/eval_jaxpr/qhd,khd->hqk/dot_general | solution.py:50
  89.7 4.0 %copy-done = f32[512,5120]{1,0:T(8,128)} copy-done((f32[512,5120]{1,0:T(8,128)}, f32[512,5120]{1,0:T(8,128)S(1)}, u32[]{:S(2)}) %copy-start) | copy-done | bytes 10485784 | tf_op jit(solution)/shard_map/while
  95.3 7.9 %fusion.65 = f32[5120,1,128]{0,2,1:T(8,128)} fusion(f32[5120,1,128]{0,2,1:T(8,128)} %get-tuple-element.337, pred[]{:T(512)S(6)} %compare.3, bf16[4,512,1,128]{3,1,2,0:T(8,128)(2,1)S(1)} %copy-done.9, s32[]{:T(128)} %get-tuple-element.335, f32[512,5120]{1,0:T(8,128)} %copy-done, f32[512]{0:T(512)S(1)} %fusion.63, f32[512]{0:T(512)S(1)} %get-tuple-element.319), kind=kOutput, calls=%fused_computation.11.clone.1 | convolution fusion | flops 680263680 | bytes 15863813 | tf_op jit(solution)/shard_map/while/body/eval_jaxpr/hqk,qhd->khd/dot_general | solution.py:75
  103.2 3.1 multiply_reduce_fusion.2
  106.3 3.6 %multiply_convert_fusion.2 = bf16[512,5120]{1,0:T(8,128)(2,1)S(1)} fusion(f32[512,5120]{1,0:T(8,128)S(1)} %get-tuple-element.320, f32[512]{0:T(512)S(1)} %get-tuple-element.321, f32[512]{0:T(512)S(1)} %fusion.63, f32[512,5120]{1,0:T(8,128)S(1)} %copy-done.1, f32[512]{0:T(512)S(1)} %get-tuple-element.319), kind=kLoop, calls=%fused_computation.2.clone.1 | loop fusion | flops 13107200 | bytes 26220544 | tf_op jit(solution)/shard_map/while/body/eval_jaxpr/convert_element_type | solution.py:65
  110.0 2.4 fusion.64
  112.4 2.2 fusion.66
  117.2 4.6 %fusion.62 = (f32[512]{0:T(512)S(1)}, f32[512,5120]{1,0:T(8,128)S(1)}) fusion(bf16[5120,1,128]{2,0,1:T(8,128)(2,1)} %get-tuple-element.356, bf16[4,512,1,128]{3,1,2,0:T(8,128)(2,1)} %get-tuple-element.352, s32[]{:T(128)} %get-tuple-element.335, pred[5120]{0:T(1024)(128)(4,1)S(1)} %get-tuple-element.316, s32[512]{0:T(512)S(1)} %iota_add_fusion.4, ...), kind=kOutput, calls=%fused_computation.57.clone.1 | convolution fusion | flops 686816768 | bytes 11968000 | tf_op jit(solution)/shard_map/while/body/eval_jaxpr/qhd,khd->hqk/dot_general | solution.py:50
  121.8 4.0 %copy-done = f32[512,5120]{1,0:T(8,128)} copy-done((f32[512,5120]{1,0:T(8,128)}, f32[512,5120]{1,0:T(8,128)S(1)}, u32[]{:S(2)}) %copy-start) | copy-done | bytes 10485784 | tf_op jit(solution)/shard_map/while
  125.8 1.6 fusion.63
  127.4 8.7 %fusion.65 = f32[5120,1,128]{0,2,1:T(8,128)} fusion(f32[5120,1,128]{0,2,1:T(8,128)} %get-tuple-element.337, pred[]{:T(512)S(6)} %compare.3, bf16[4,512,1,128]{3,1,2,0:T(8,128)(2,1)S(1)} %copy-done.9, s32[]{:T(128)} %get-tuple-element.335, f32[512,5120]{1,0:T(8,128)} %copy-done, f32[512]{0:T(512)S(1)} %fusion.63, f32[512]{0:T(512)S(1)} %get-tuple-element.319), kind=kOutput, calls=%fused_computation.11.clone.1 | convolution fusion | flops 680263680 | bytes 15863813 | tf_op jit(solution)/shard_map/while/body/eval_jaxpr/hqk,qhd->khd/dot_general | solution.py:75
  136.0 3.1 multiply_reduce_fusion.2
  139.2 3.6 %multiply_convert_fusion.2 = bf16[512,5120]{1,0:T(8,128)(2,1)S(1)} fusion(f32[512,5120]{1,0:T(8,128)S(1)} %get-tuple-element.320, f32[512]{0:T(512)S(1)} %get-tuple-element.321, f32[512]{0:T(512)S(1)} %fusion.63, f32[512,5120]{1,0:T(8,128)S(1)} %copy-done.1, f32[512]{0:T(512)S(1)} %get-tuple-element.319), kind=kLoop, calls=%fused_computation.2.clone.1 | loop fusion | flops 13107200 | bytes 26220544 | tf_op jit(solution)/shard_map/while/body/eval_jaxpr/convert_element_type | solution.py:65
  142.8 2.4 fusion.64
  145.3 2.2 fusion.66
  150.1 4.6 %fusion.62 = (f32[512]{0:T(512)S(1)}, f32[512,5120]{1,0:T(8,128)S(1)}) fusion(bf16[5120,1,128]{2,0,1:T(8,128)(2,1)} %get-tuple-element.356, bf16[4,512,1,128]{3,1,2,0:T(8,128)(2,1)} %get-tuple-element.352, s32[]{:T(128)} %get-tuple-element.335, pred[5120]{0:T(1024)(128)(4,1)S(1)} %get-tuple-element.316, s32[512]{0:T(512)S(1)} %iota_add_fusion.4, ...), kind=kOutput, calls=%fused_computation.57.clone.1 | convolution fusion | flops 686816768 | bytes 11968000 | tf_op jit(solution)/shard_map/while/body/eval_jaxpr/qhd,khd->hqk/dot_general | solution.py:50
  154.7 4.0 %copy-done = f32[512,5120]{1,0:T(8,128)} copy-done((f32[512,5120]{1,0:T(8,128)}, f32[512,5120]{1,0:T(8,128)S(1)}, u32[]{:S(2)}) %copy-start) | copy-done | bytes 10485784 | tf_op jit(solution)/shard_map/while
  160.2 8.7 %fusion.65 = f32[5120,1,128]{0,2,1:T(8,128)} fusion(f32[5120,1,128]{0,2,1:T(8,128)} %get-tuple-element.337, pred[]{:T(512)S(6)} %compare.3, bf16[4,512,1,128]{3,1,2,0:T(8,128)(2,1)S(1)} %copy-done.9, s32[]{:T(128)} %get-tuple-element.335, f32[512,5120]{1,0:T(8,128)} %copy-done, f32[512]{0:T(512)S(1)} %fusion.63, f32[512]{0:T(512)S(1)} %get-tuple-element.319), kind=kOutput, calls=%fused_computation.11.clone.1 | convolution fusion | flops 680263680 | bytes 15863813 | tf_op jit(solution)/shard_map/while/body/eval_jaxpr/hqk,qhd->khd/dot_general | solution.py:75
  168.9 3.1 multiply_reduce_fusion.2
  172.0 3.6 %multiply_convert_fusion.2 = bf16[512,5120]{1,0:T(8,128)(2,1)S(1)} fusion(f32[512,5120]{1,0:T(8,128)S(1)} %get-tuple-element.320, f32[512]{0:T(512)S(1)} %get-tuple-element.321, f32[512]{0:T(512)S(1)} %fusion.63, f32[512,5120]{1,0:T(8,128)S(1)} %copy-done.1, f32[512]{0:T(512)S(1)} %get-tuple-element.319), kind=kLoop, calls=%fused_computation.2.clone.1 | loop fusion | flops 13107200 | bytes 26220544 | tf_op jit(solution)/shard_map/while/body/eval_jaxpr/convert_element_type | solution.py:65
  175.7 2.4 fusion.64
  178.1 2.2 fusion.66
  182.9 4.6 %fusion.62 = (f32[512]{0:T(512)S(1)}, f32[512,5120]{1,0:T(8,128)S(1)}) fusion(bf16[5120,1,128]{2,0,1:T(8,128)(2,1)} %get-tuple-element.356, bf16[4,512,1,128]{3,1,2,0:T(8,128)(2,1)} %get-tuple-element.352, s32[]{:T(128)} %get-tuple-element.335, pred[5120]{0:T(1024)(128)(4,1)S(1)} %get-tuple-element.316, s32[512]{0:T(512)S(1)} %iota_add_fusion.4, ...), kind=kOutput, calls=%fused_computation.57.clone.1 | convolution fusion | flops 686816768 | bytes 11968000 | tf_op jit(solution)/shard_map/while/body/eval_jaxpr/qhd,khd->hqk/dot_general | solution.py:50
  187.5 4.0 %copy-done = f32[512,5120]{1,0:T(8,128)} copy-done((f32[512,5120]{1,0:T(8,128)}, f32[512,5120]{1,0:T(8,128)S(1)}, u32[]{:S(2)}) %copy-start) | copy-done | bytes 10485784 | tf_op jit(solution)/shard_map/while
  193.1 8.7 %fusion.65 = f32[5120,1,128]{0,2,1:T(8,128)} fusion(f32[5120,1,128]{0,2,1:T(8,128)} %get-tuple-element.337, pred[]{:T(512)S(6)} %compare.3, bf16[4,512,1,128]{3,1,2,0:T(8,128)(2,1)S(1)} %copy-done.9, s32[]{:T(128)} %get-tuple-element.335, f32[512,5120]{1,0:T(8,128)} %copy-done, f32[512]{0:T(512)S(1)} %fusion.63, f32[512]{0:T(512)S(1)} %get-tuple-element.319), kind=kOutput, calls=%fused_computation.11.clone.1 | convolution fusion | flops 680263680 | bytes 15863813 | tf_op jit(solution)/shard_map/while/body/eval_jaxpr/hqk,qhd->khd/dot_general | solution.py:75
  201.8 3.1 multiply_reduce_fusion.2
  204.9 3.6 %multiply_convert_fusion.2 = bf16[512,5120]{1,0:T(8,128)(2,1)S(1)} fusion(f32[512,5120]{1,0:T(8,128)S(1)} %get-tuple-element.320, f32[512]{0:T(512)S(1)} %get-tuple-element.321, f32[512]{0:T(512)S(1)} %fusion.63, f32[512,5120]{1,0:T(8,128)S(1)} %copy-done.1, f32[512]{0:T(512)S(1)} %get-tuple-element.319), kind=kLoop, calls=%fused_computation.2.clone.1 | loop fusion | flops 13107200 | bytes 26220544 | tf_op jit(solution)/shard_map/while/body/eval_jaxpr/convert_element_type | solution.py:65
  208.5 2.4 fusion.64
  211.0 2.2 fusion.66
  213.2 2.1 copy.56
  215.3 2.1 fusion.40
  217.3 2.2 copy.57
  220.8 10.0 %copy.58 = bf16[2048,3,1,128]{3,1,2,0:T(4,128)(2,1)S(1)} copy(bf16[2048,3,1,128]{3,0,2,1:T(8,128)(2,1)S(1)} %pad_maximum_fusion) | data formatting | bytes 3145728 | tf_op jit(solution)/shard_map/stack | solution.py:98
  230.8 56.5 %all_to_all.51 = bf16[2048,3,1,128]{3,1,2,0:T(4,128)(2,1)S(1)} all-to-all(bf16[2048,3,1,128]{3,1,2,0:T(4,128)(2,1)S(1)} %copy.58), channel_id=1, replica_groups=mesh['section'=4,'seq'=64] {'seq'}, dimensions={0} | all-to-all | bytes 3145728 | tf_op jit(solution)/shard_map/all_to_all | solution.py:106
  289.9 5.0 %maximum_add_fusion = f32[1,3072,2,1,128]{4,3,2,1,0:T(1,128)} fusion(f32[1,3072,2,1,128]{4,3,2,1,0:T(1,128)S(1)} %copy-done.3, f32[1,3072,1,1,128]{4,3,2,1,0:T(1,128)S(1)} %bitcast.146, f32[1,3072,1,1,128]{4,3,2,1,0:T(1,128)S(1)} %bitcast.143), kind=kLoop, calls=%fused_computation.40 | loop fusion | flops 1572864 | bytes 9437184 | tf_op jit(solution)/shard_map/add | solution.py:97
  294.9 30.1 %collective-permute-done = bf16[32,3,64,128]{3,0,2,1:T(8,128)(2,1)S(1)} collective-permute-done((bf16[32,3,64,128]{3,0,2,1:T(8,128)(2,1)S(1)}, bf16[32,3,64,128]{3,0,2,1:T(8,128)(2,1)S(1)}, u32[]{:S(2)}, u32[]{:S(2)}) %collective-permute-start) | collective-permute-done | bytes 1572896 | tf_op jit(solution)/shard_map/ppermute | solution.py:14
  325.6 2.1 reshape.128
  (86 shorter events, 25.1 us)
Async XLA Ops:
  0.6 14.0 %copy-start.6 = (bf16[1,32,3,8192]{3,1,2,0:T(8,128)(2,1)S(1)}, bf16[1,32,3,8192]{3,1,2,0:T(8,128)(2,1)}, u32[]{:S(2)}) copy-start(bf16[1,32,3,8192]{3,1,2,0:T(8,128)(2,1)} %param.8) | copy-start | bytes 4718596
  3.1 28.3 %all-to-all-start.1 = ((bf16[32,1,64,128]{3,0,1,2:T(8,128)(2,1)}), bf16[32,1,64,128]{3,0,1,2:T(8,128)(2,1)S(1)}, u32[]{:S(2)}, u32[]{:S(2)}) async-start(bf16[32,1,64,128]{3,0,1,2:T(8,128)(2,1)} %copy.52), calls=%async_computation.1 | async-start | bytes 1048576 | tf_op jit(solution)/shard_map/all_to_all | solution.py:28
  31.3 0.8 copy-start.4
  32.2 46.0 %all-to-all-start = ((bf16[32,3,64,128]{3,0,1,2:T(8,128)(2,1)}), bf16[32,3,64,128]{3,0,1,2:T(8,128)(2,1)}, u32[]{:S(2)}, u32[]{:S(2)}) async-start(bf16[32,3,64,128]{3,0,1,2:T(8,128)(2,1)} %copy.49), calls=%async_computation | async-start | bytes 3145728 | tf_op jit(solution)/shard_map/all_to_all | solution.py:27
  78.1 2.7 copy-start.2
  89.7 4.0 %copy-start = (f32[512,5120]{1,0:T(8,128)}, f32[512,5120]{1,0:T(8,128)S(1)}, u32[]{:S(2)}) copy-start(f32[512,5120]{1,0:T(8,128)S(1)} %get-tuple-element.318) | copy-start | bytes 31457284 | tf_op jit(solution)/shard_map/while
  93.7 1.6 copy-start.9
  95.2 7.9 %copy-start.1 = (f32[512,5120]{1,0:T(8,128)S(1)}, f32[512,5120]{1,0:T(8,128)}, u32[]{:S(2)}) copy-start(f32[512,5120]{1,0:T(8,128)} %copy-done) | copy-start | bytes 31457284 | tf_op jit(solution)/shard_map/while
  95.3 7.9 %copy-start.8 = (bf16[5120,1,128]{2,0,1:T(8,128)(2,1)S(1)}, bf16[5120,1,128]{2,0,1:T(8,128)(2,1)}, u32[]{:S(2)}) copy-start(bf16[5120,1,128]{2,0,1:T(8,128)(2,1)} %get-tuple-element.358) | copy-start | bytes 3932164 | tf_op jit(solution)/shard_map/while
  109.9 2.5 copy-start.7
  121.8 4.0 %copy-start = (f32[512,5120]{1,0:T(8,128)}, f32[512,5120]{1,0:T(8,128)S(1)}, u32[]{:S(2)}) copy-start(f32[512,5120]{1,0:T(8,128)S(1)} %get-tuple-element.318) | copy-start | bytes 31457284 | tf_op jit(solution)/shard_map/while
  125.8 1.6 copy-start.9
  127.4 8.7 %copy-start.1 = (f32[512,5120]{1,0:T(8,128)S(1)}, f32[512,5120]{1,0:T(8,128)}, u32[]{:S(2)}) copy-start(f32[512,5120]{1,0:T(8,128)} %copy-done) | copy-start | bytes 31457284 | tf_op jit(solution)/shard_map/while
  127.4 8.7 %copy-start.8 = (bf16[5120,1,128]{2,0,1:T(8,128)(2,1)S(1)}, bf16[5120,1,128]{2,0,1:T(8,128)(2,1)}, u32[]{:S(2)}) copy-start(bf16[5120,1,128]{2,0,1:T(8,128)(2,1)} %get-tuple-element.358) | copy-start | bytes 3932164 | tf_op jit(solution)/shard_map/while
  142.8 2.5 copy-start.7
  154.6 4.0 %copy-start = (f32[512,5120]{1,0:T(8,128)}, f32[512,5120]{1,0:T(8,128)S(1)}, u32[]{:S(2)}) copy-start(f32[512,5120]{1,0:T(8,128)S(1)} %get-tuple-element.318) | copy-start | bytes 31457284 | tf_op jit(solution)/shard_map/while
  158.6 1.6 copy-start.9
  160.2 8.7 %copy-start.1 = (f32[512,5120]{1,0:T(8,128)S(1)}, f32[512,5120]{1,0:T(8,128)}, u32[]{:S(2)}) copy-start(f32[512,5120]{1,0:T(8,128)} %copy-done) | copy-start | bytes 31457284 | tf_op jit(solution)/shard_map/while
  160.2 8.7 %copy-start.8 = (bf16[5120,1,128]{2,0,1:T(8,128)(2,1)S(1)}, bf16[5120,1,128]{2,0,1:T(8,128)(2,1)}, u32[]{:S(2)}) copy-start(bf16[5120,1,128]{2,0,1:T(8,128)(2,1)} %get-tuple-element.358) | copy-start | bytes 3932164 | tf_op jit(solution)/shard_map/while
  175.7 2.5 copy-start.7
  187.5 4.0 %copy-start = (f32[512,5120]{1,0:T(8,128)}, f32[512,5120]{1,0:T(8,128)S(1)}, u32[]{:S(2)}) copy-start(f32[512,5120]{1,0:T(8,128)S(1)} %get-tuple-element.318) | copy-start | bytes 31457284 | tf_op jit(solution)/shard_map/while
  191.5 1.6 copy-start.9
  193.1 8.7 %copy-start.1 = (f32[512,5120]{1,0:T(8,128)S(1)}, f32[512,5120]{1,0:T(8,128)}, u32[]{:S(2)}) copy-start(f32[512,5120]{1,0:T(8,128)} %copy-done) | copy-start | bytes 31457284 | tf_op jit(solution)/shard_map/while
  193.1 8.7 %copy-start.8 = (bf16[5120,1,128]{2,0,1:T(8,128)(2,1)S(1)}, bf16[5120,1,128]{2,0,1:T(8,128)(2,1)}, u32[]{:S(2)}) copy-start(bf16[5120,1,128]{2,0,1:T(8,128)(2,1)} %get-tuple-element.358) | copy-start | bytes 3932164 | tf_op jit(solution)/shard_map/while
  208.5 2.5 copy-start.7
  217.3 2.3 copy-start.5
  287.5 1.4 slice-start
  287.5 2.4 copy-start.3
  287.5 37.5 %collective-permute-start = (bf16[32,3,64,128]{3,0,2,1:T(8,128)(2,1)S(1)}, bf16[32,3,64,128]{3,0,2,1:T(8,128)(2,1)S(1)}, u32[]{:S(2)}, u32[]{:S(2)}) collective-permute-start(bf16[32,3,64,128]{3,0,2,1:T(8,128)(2,1)S(1)} %bitcast.152), channel_id=1, source_target_pairs={{64,0},{128,64},{192,128},{0,192},{65,1},{129,65},{193,129},{1,193... | collective-permute-start | bytes 4718600 | tf_op jit(solution)/shard_map/ppermute | solution.py:14
where the time goes:
time: 329 us; the launch traced here: 328 us
  matrix products  83.2 us (25%)
  waiting for transfers between devices  74.4 us (23%)
  blocking collectives  56.5 us (17%)
  local copies, waits for them, and re-layouts  53.9 us (16%)
  other arithmetic  38.6 us (12%)
  starting transfers between devices  19.3 us (6%)
    all_to_all x1, blocking collectives, per_device(): lax.all_to_all(span_grads, 'seq', split_axis=0, concat_axis=2, tiled=True)  56.5 us
    dot_general x4, matrix products, backward_block(): jnp.einsum('hqk,qhd->khd', attention_low, dout_block, preferred_element_t...  33.9 us
    all_to_all x1, waiting for transfers between devices, per_device(): lax.all_to_all(local_rows, 'seq', split_axis=2, concat_axis=0, tiled=True)  30.2 us
    ppermute x1, waiting for transfers between devices, from_behind(): return lax.ppermute(block, axis, route)  30.1 us
    dot_general x4, matrix products, scores(): jnp.einsum('qhd,khd->hqk', query_block, all_keys, preferred_element_type=...  18.3 us
    while x40, local copies, waits for them, and re-layouts  16 us
    convert_element_type x4, other arithmetic, backward_block(): dscores = (attention * (dprobs - row_delta)).astype(jnp.bfloat16)  14.5 us
    all_to_all x1, waiting for transfers between devices, per_device(): lax.all_to_all(upstream, 'seq', split_axis=2, concat_axis=0, tiled=True)  14.1 us
  transfers between devices with their start and end apart: 3, of which 3 were waited for; matrix products, arithmetic and copies ran while one was open for 5% of the time, Pallas kernels for 0%

commit v1 on v0

--- a/solution.py
+++ b/solution.py
@@ -103,7 +103,10 @@
         ],
         axis=1,
     )
-    regrouped = lax.all_to_all(span_grads, "seq", split_axis=0, concat_axis=2, tiled=True)
+    regrouped = jnp.concatenate(
+        lax.all_to_all(jnp.stack(jnp.split(span_grads, lax.axis_size("seq"), axis=0)), "seq", 0, 0),
+        axis=2,
+    )
     moved = from_behind(regrouped, "section", -1)
     return (moved.reshape(1, tok_rows, 3, HEADS * DH), new_accum[None])
 

time: 329 us -> 309 us (0.939)
  blocking collectives: 56.5 us -> 45.2 us
  local copies, waits for them, and re-layouts: 53.9 us -> 45.7 us
    all_to_all x1, blocking collectives: 56.5 us -> 45.2 us  [per_device(): lax.all_to_all(jnp.stack(jnp.split(span_grads, lax.axis_size('seq'), axis...]
    another operation x3 -> x2, local copies, waits for them, and re-layouts: 12.1 us -> 2.12 us  [per_device(): jnp.stack([grad_query.reshape(span_len, local_heads, DH), grad_keys[past_...]
    unnamed x14 -> x79, local copies, waits for them, and re-layouts: 7.13 us -> 8.91 us
where the time goes in v1:
time: 309 us; the launch traced here: 308 us
  matrix products  83.2 us (27%)
  waiting for transfers between devices  74.7 us (24%)
  local copies, waits for them, and re-layouts  45.7 us (15%)
  blocking collectives  45.2 us (15%)
  other arithmetic  37.7 us (12%)
  starting transfers between devices  19.3 us (6%)
    all_to_all x1, blocking collectives, per_device(): lax.all_to_all(jnp.stack(jnp.split(span_grads, lax.axis_size('seq'), axis...  45.2 us
    dot_general x4, matrix products, backward_block(): jnp.einsum('hqk,qhd->khd', attention_low, dout_block, preferred_element_t...  33.9 us
    all_to_all x1, waiting for transfers between devices, per_device(): lax.all_to_all(local_rows, 'seq', split_axis=2, concat_axis=0, tiled=True)  31.2 us
    ppermute x1, waiting for transfers between devices, from_behind(): return lax.ppermute(block, axis, route)  29.5 us
    dot_general x4, matrix products, scores(): jnp.einsum('qhd,khd->hqk', query_block, all_keys, preferred_element_type=...  18.3 us
    while x40, local copies, waits for them, and re-layouts  16 us
    convert_element_type x4, other arithmetic, backward_block(): dscores = (attention * (dprobs - row_delta)).astype(jnp.bfloat16)  14.5 us
    all_to_all x1, waiting for transfers between devices, per_device(): lax.all_to_all(upstream, 'seq', split_axis=2, concat_axis=0, tiled=True)  14.1 us
  transfers between devices with their start and end apart: 3, of which 3 were waited for; matrix products, arithmetic and copies ran while one was open for 5% of the time, Pallas kernels for 0%

profile of v1, /device:TPU:56, one launch (start us, length us, event | category | flops | bytes accessed | tf_op | source)
XLA Modules:
  0.0 307.8 jit_solution(17523351807792778259)
XLA Ops:
  3.1 11.6 %all-to-all-start.1 = ((bf16[32,1,64,128]{3,0,1,2:T(8,128)(2,1)}), bf16[32,1,64,128]{3,0,1,2:T(8,128)(2,1)S(1)}, u32[]{:S(2)}, u32[]{:S(2)}) async-start(bf16[32,1,64,128]{3,0,1,2:T(8,128)(2,1)} %copy.303), calls=%async_computation.1 | async-start | bytes 1048576 | tf_op jit(solution)/shard_map/all_to_all | solution.py:28
  15.1 2.2 copy.300
  17.3 14.1 %all-to-all-done.1 = bf16[32,1,64,128]{3,0,1,2:T(8,128)(2,1)S(1)} async-done(((bf16[32,1,64,128]{3,0,1,2:T(8,128)(2,1)}), bf16[32,1,64,128]{3,0,1,2:T(8,128)(2,1)S(1)}, u32[]{:S(2)}, u32[]{:S(2)}) %all-to-all-start.1) | async-done | bytes 524320 | tf_op jit(solution)/shard_map/all_to_all | solution.py:28
  32.1 6.9 %all-to-all-start = ((bf16[32,3,64,128]{3,0,1,2:T(8,128)(2,1)}), bf16[32,3,64,128]{3,0,1,2:T(8,128)(2,1)}, u32[]{:S(2)}, u32[]{:S(2)}) async-start(bf16[32,3,64,128]{3,0,1,2:T(8,128)(2,1)} %copy.300), calls=%async_computation | async-start | bytes 3145728 | tf_op jit(solution)/shard_map/all_to_all | solution.py:27
  39.0 2.8 copy.379
  43.3 2.4 slice_bitcast_fusion
  46.9 31.2 %all-to-all-done = bf16[32,3,64,128]{3,0,1,2:T(8,128)(2,1)} async-done(((bf16[32,3,64,128]{3,0,1,2:T(8,128)(2,1)}), bf16[32,3,64,128]{3,0,1,2:T(8,128)(2,1)}, u32[]{:S(2)}, u32[]{:S(2)}) %all-to-all-start) | async-done | bytes 1572896 | tf_op jit(solution)/shard_map/all_to_all | solution.py:27
  78.1 1.7 copy.301
  81.1 1.7 pad_maximum_fusion.1
  82.8 130.6 %while.16 = (s32[]{:T(128)}, f32[5120,1,128]{0,2,1:T(8,128)S(1)}, f32[5120,1,128]{0,2,1:T(8,128)}, bf16[4,512,1,128]{3,1,2,0:T(8,128)(2,1)}, bf16[4,512,1,128]{3...) while((s32[]{:T(128)}, f32[5120,1,128]{0,2,1:T(8,128)S(1)}, ...), condition=%wide.region_4.5_spmd.clone.clone, body=%wide.region_0.4_spmd.clone.clone.sunk | while | flops 3411304448 | bytes 200771376 | solution.py:94
  85.3 4.6 %fusion.62 = (f32[512]{0:T(512)S(1)}, f32[512,5120]{1,0:T(8,128)S(1)}) fusion(bf16[5120,1,128]{2,0,1:T(8,128)(2,1)} %get-tuple-element.358, bf16[4,512,1,128]{3,1,2,0:T(8,128)(2,1)} %get-tuple-element.354, s32[]{:T(128)} %get-tuple-element.337, pred[5120]{0:T(1024)(128)(4,1)S(1)} %get-tuple-element.318, s32[512]{0:T(512)S(1)} %iota_add_fusion.4, ...), kind=kOutput, calls=%fused_computation.185.clone.1 | convolution fusion | flops 686816768 | bytes 11968000 | tf_op jit(solution)/shard_map/while/body/eval_jaxpr/qhd,khd->hqk/dot_general | solution.py:50
  89.9 4.0 %copy-done = f32[512,5120]{1,0:T(8,128)} copy-done((f32[512,5120]{1,0:T(8,128)}, f32[512,5120]{1,0:T(8,128)S(1)}, u32[]{:S(2)}) %copy-start) | copy-done | bytes 10485784 | tf_op jit(solution)/shard_map/while
  93.9 1.6 fusion.63
  95.5 7.9 %fusion.65 = f32[5120,1,128]{0,2,1:T(8,128)} fusion(f32[5120,1,128]{0,2,1:T(8,128)} %get-tuple-element.339, pred[]{:T(512)S(6)} %compare.3, bf16[4,512,1,128]{3,1,2,0:T(8,128)(2,1)S(1)} %copy-done.10, s32[]{:T(128)} %get-tuple-element.337, f32[512,5120]{1,0:T(8,128)} %copy-done, f32[512]{0:T(512)S(1)} %fusion.63, f32[512]{0:T(512)S(1)} %get-tuple-element.321), kind=kOutput, calls=%fused_computation.11.clone.1 | convolution fusion | flops 680263680 | bytes 15863813 | tf_op jit(solution)/shard_map/while/body/eval_jaxpr/hqk,qhd->khd/dot_general | solution.py:75
  103.4 3.1 %multiply_reduce_fusion.2 = (f32[512]{0:T(512)S(1)}, f32[512,5120]{1,0:T(8,128)S(1)}) fusion(f32[512]{0:T(512)S(1)} %fusion.63, f32[512,5120]{1,0:T(8,128)S(1)} %copy-done.1, f32[512]{0:T(512)S(1)} %get-tuple-element.321, bf16[5120,1,128]{2,0,1:T(8,128)(2,1)S(1)} %copy-done.9, bf16[4,512,1,128]{3,1,2,0:T(8,128)(2,1)S(1)} %copy-done.10, ...), kind=kOutput, calls=%fused_computation.3.clone.1 | convolution fusion | flops 681573888 | bytes 22419460 | tf_op jit(solution)/shard_map/while/body/eval_jaxpr/qhd,khd->hqk/dot_general | solution.py:61
  106.6 3.6 %multiply_convert_fusion.2 = bf16[512,5120]{1,0:T(8,128)(2,1)S(1)} fusion(f32[512,5120]{1,0:T(8,128)S(1)} %get-tuple-element.322, f32[512]{0:T(512)S(1)} %get-tuple-element.323, f32[512]{0:T(512)S(1)} %fusion.63, f32[512,5120]{1,0:T(8,128)S(1)} %copy-done.1, f32[512]{0:T(512)S(1)} %get-tuple-element.321), kind=kLoop, calls=%fused_computation.2.clone.1 | loop fusion | flops 13107200 | bytes 26220544 | tf_op jit(solution)/shard_map/while/body/eval_jaxpr/convert_element_type | solution.py:65
  110.2 2.4 fusion.64
  112.7 2.2 fusion.66
  117.4 4.6 %fusion.62 = (f32[512]{0:T(512)S(1)}, f32[512,5120]{1,0:T(8,128)S(1)}) fusion(bf16[5120,1,128]{2,0,1:T(8,128)(2,1)} %get-tuple-element.358, bf16[4,512,1,128]{3,1,2,0:T(8,128)(2,1)} %get-tuple-element.354, s32[]{:T(128)} %get-tuple-element.337, pred[5120]{0:T(1024)(128)(4,1)S(1)} %get-tuple-element.318, s32[512]{0:T(512)S(1)} %iota_add_fusion.4, ...), kind=kOutput, calls=%fused_computation.185.clone.1 | convolution fusion | flops 686816768 | bytes 11968000 | tf_op jit(solution)/shard_map/while/body/eval_jaxpr/qhd,khd->hqk/dot_general | solution.py:50
  122.0 4.0 %copy-done = f32[512,5120]{1,0:T(8,128)} copy-done((f32[512,5120]{1,0:T(8,128)}, f32[512,5120]{1,0:T(8,128)S(1)}, u32[]{:S(2)}) %copy-start) | copy-done | bytes 10485784 | tf_op jit(solution)/shard_map/while
  127.6 8.7 %fusion.65 = f32[5120,1,128]{0,2,1:T(8,128)} fusion(f32[5120,1,128]{0,2,1:T(8,128)} %get-tuple-element.339, pred[]{:T(512)S(6)} %compare.3, bf16[4,512,1,128]{3,1,2,0:T(8,128)(2,1)S(1)} %copy-done.10, s32[]{:T(128)} %get-tuple-element.337, f32[512,5120]{1,0:T(8,128)} %copy-done, f32[512]{0:T(512)S(1)} %fusion.63, f32[512]{0:T(512)S(1)} %get-tuple-element.321), kind=kOutput, calls=%fused_computation.11.clone.1 | convolution fusion | flops 680263680 | bytes 15863813 | tf_op jit(solution)/shard_map/while/body/eval_jaxpr/hqk,qhd->khd/dot_general | solution.py:75
  136.3 3.1 %multiply_reduce_fusion.2 = (f32[512]{0:T(512)S(1)}, f32[512,5120]{1,0:T(8,128)S(1)}) fusion(f32[512]{0:T(512)S(1)} %fusion.63, f32[512,5120]{1,0:T(8,128)S(1)} %copy-done.1, f32[512]{0:T(512)S(1)} %get-tuple-element.321, bf16[5120,1,128]{2,0,1:T(8,128)(2,1)S(1)} %copy-done.9, bf16[4,512,1,128]{3,1,2,0:T(8,128)(2,1)S(1)} %copy-done.10, ...), kind=kOutput, calls=%fused_computation.3.clone.1 | convolution fusion | flops 681573888 | bytes 22419460 | tf_op jit(solution)/shard_map/while/body/eval_jaxpr/qhd,khd->hqk/dot_general | solution.py:61
  139.4 3.6 %multiply_convert_fusion.2 = bf16[512,5120]{1,0:T(8,128)(2,1)S(1)} fusion(f32[512,5120]{1,0:T(8,128)S(1)} %get-tuple-element.322, f32[512]{0:T(512)S(1)} %get-tuple-element.323, f32[512]{0:T(512)S(1)} %fusion.63, f32[512,5120]{1,0:T(8,128)S(1)} %copy-done.1, f32[512]{0:T(512)S(1)} %get-tuple-element.321), kind=kLoop, calls=%fused_computation.2.clone.1 | loop fusion | flops 13107200 | bytes 26220544 | tf_op jit(solution)/shard_map/while/body/eval_jaxpr/convert_element_type | solution.py:65
  143.0 2.4 fusion.64
  145.5 2.2 fusion.66
  150.2 4.6 %fusion.62 = (f32[512]{0:T(512)S(1)}, f32[512,5120]{1,0:T(8,128)S(1)}) fusion(bf16[5120,1,128]{2,0,1:T(8,128)(2,1)} %get-tuple-element.358, bf16[4,512,1,128]{3,1,2,0:T(8,128)(2,1)} %get-tuple-element.354, s32[]{:T(128)} %get-tuple-element.337, pred[5120]{0:T(1024)(128)(4,1)S(1)} %get-tuple-element.318, s32[512]{0:T(512)S(1)} %iota_add_fusion.4, ...), kind=kOutput, calls=%fused_computation.185.clone.1 | convolution fusion | flops 686816768 | bytes 11968000 | tf_op jit(solution)/shard_map/while/body/eval_jaxpr/qhd,khd->hqk/dot_general | solution.py:50
  154.8 4.0 %copy-done = f32[512,5120]{1,0:T(8,128)} copy-done((f32[512,5120]{1,0:T(8,128)}, f32[512,5120]{1,0:T(8,128)S(1)}, u32[]{:S(2)}) %copy-start) | copy-done | bytes 10485784 | tf_op jit(solution)/shard_map/while
  160.4 8.7 %fusion.65 = f32[5120,1,128]{0,2,1:T(8,128)} fusion(f32[5120,1,128]{0,2,1:T(8,128)} %get-tuple-element.339, pred[]{:T(512)S(6)} %compare.3, bf16[4,512,1,128]{3,1,2,0:T(8,128)(2,1)S(1)} %copy-done.10, s32[]{:T(128)} %get-tuple-element.337, f32[512,5120]{1,0:T(8,128)} %copy-done, f32[512]{0:T(512)S(1)} %fusion.63, f32[512]{0:T(512)S(1)} %get-tuple-element.321), kind=kOutput, calls=%fused_computation.11.clone.1 | convolution fusion | flops 680263680 | bytes 15863813 | tf_op jit(solution)/shard_map/while/body/eval_jaxpr/hqk,qhd->khd/dot_general | solution.py:75
  169.1 3.1 %multiply_reduce_fusion.2 = (f32[512]{0:T(512)S(1)}, f32[512,5120]{1,0:T(8,128)S(1)}) fusion(f32[512]{0:T(512)S(1)} %fusion.63, f32[512,5120]{1,0:T(8,128)S(1)} %copy-done.1, f32[512]{0:T(512)S(1)} %get-tuple-element.321, bf16[5120,1,128]{2,0,1:T(8,128)(2,1)S(1)} %copy-done.9, bf16[4,512,1,128]{3,1,2,0:T(8,128)(2,1)S(1)} %copy-done.10, ...), kind=kOutput, calls=%fused_computation.3.clone.1 | convolution fusion | flops 681573888 | bytes 22419460 | tf_op jit(solution)/shard_map/while/body/eval_jaxpr/qhd,khd->hqk/dot_general | solution.py:61
  172.2 3.6 %multiply_convert_fusion.2 = bf16[512,5120]{1,0:T(8,128)(2,1)S(1)} fusion(f32[512,5120]{1,0:T(8,128)S(1)} %get-tuple-element.322, f32[512]{0:T(512)S(1)} %get-tuple-element.323, f32[512]{0:T(512)S(1)} %fusion.63, f32[512,5120]{1,0:T(8,128)S(1)} %copy-done.1, f32[512]{0:T(512)S(1)} %get-tuple-element.321), kind=kLoop, calls=%fused_computation.2.clone.1 | loop fusion | flops 13107200 | bytes 26220544 | tf_op jit(solution)/shard_map/while/body/eval_jaxpr/convert_element_type | solution.py:65
  175.8 2.4 fusion.64
  178.3 2.2 fusion.66
  183.1 4.6 %fusion.62 = (f32[512]{0:T(512)S(1)}, f32[512,5120]{1,0:T(8,128)S(1)}) fusion(bf16[5120,1,128]{2,0,1:T(8,128)(2,1)} %get-tuple-element.358, bf16[4,512,1,128]{3,1,2,0:T(8,128)(2,1)} %get-tuple-element.354, s32[]{:T(128)} %get-tuple-element.337, pred[5120]{0:T(1024)(128)(4,1)S(1)} %get-tuple-element.318, s32[512]{0:T(512)S(1)} %iota_add_fusion.4, ...), kind=kOutput, calls=%fused_computation.185.clone.1 | convolution fusion | flops 686816768 | bytes 11968000 | tf_op jit(solution)/shard_map/while/body/eval_jaxpr/qhd,khd->hqk/dot_general | solution.py:50
  187.7 4.0 %copy-done = f32[512,5120]{1,0:T(8,128)} copy-done((f32[512,5120]{1,0:T(8,128)}, f32[512,5120]{1,0:T(8,128)S(1)}, u32[]{:S(2)}) %copy-start) | copy-done | bytes 10485784 | tf_op jit(solution)/shard_map/while
  191.6 1.6 fusion.63
  193.3 8.7 %fusion.65 = f32[5120,1,128]{0,2,1:T(8,128)} fusion(f32[5120,1,128]{0,2,1:T(8,128)} %get-tuple-element.339, pred[]{:T(512)S(6)} %compare.3, bf16[4,512,1,128]{3,1,2,0:T(8,128)(2,1)S(1)} %copy-done.10, s32[]{:T(128)} %get-tuple-element.337, f32[512,5120]{1,0:T(8,128)} %copy-done, f32[512]{0:T(512)S(1)} %fusion.63, f32[512]{0:T(512)S(1)} %get-tuple-element.321), kind=kOutput, calls=%fused_computation.11.clone.1 | convolution fusion | flops 680263680 | bytes 15863813 | tf_op jit(solution)/shard_map/while/body/eval_jaxpr/hqk,qhd->khd/dot_general | solution.py:75
  201.9 3.1 %multiply_reduce_fusion.2 = (f32[512]{0:T(512)S(1)}, f32[512,5120]{1,0:T(8,128)S(1)}) fusion(f32[512]{0:T(512)S(1)} %fusion.63, f32[512,5120]{1,0:T(8,128)S(1)} %copy-done.1, f32[512]{0:T(512)S(1)} %get-tuple-element.321, bf16[5120,1,128]{2,0,1:T(8,128)(2,1)S(1)} %copy-done.9, bf16[4,512,1,128]{3,1,2,0:T(8,128)(2,1)S(1)} %copy-done.10, ...), kind=kOutput, calls=%fused_computation.3.clone.1 | convolution fusion | flops 681573888 | bytes 22419460 | tf_op jit(solution)/shard_map/while/body/eval_jaxpr/qhd,khd->hqk/dot_general | solution.py:61
  205.0 3.6 %multiply_convert_fusion.2 = bf16[512,5120]{1,0:T(8,128)(2,1)S(1)} fusion(f32[512,5120]{1,0:T(8,128)S(1)} %get-tuple-element.322, f32[512]{0:T(512)S(1)} %get-tuple-element.323, f32[512]{0:T(512)S(1)} %fusion.63, f32[512,5120]{1,0:T(8,128)S(1)} %copy-done.1, f32[512]{0:T(512)S(1)} %get-tuple-element.321), kind=kLoop, calls=%fused_computation.2.clone.1 | loop fusion | flops 13107200 | bytes 26220544 | tf_op jit(solution)/shard_map/while/body/eval_jaxpr/convert_element_type | solution.py:65
  208.7 2.4 fusion.64
  211.1 2.2 fusion.66
  213.3 2.1 copy.307
  215.4 2.1 fusion.40
  217.5 2.4 copy.308
  222.1 45.2 %all_to_all.38 = bf16[64,32,3,1,128]{4,1,3,2,0:T(8,128)(2,1)S(1)} all-to-all(bf16[64,32,3,1,128]{4,1,3,2,0:T(8,128)(2,1)S(1)} %constant_dynamic-update-slice_fusion), channel_id=1, replica_groups=mesh['section'=4,'seq'=64] {'seq'}, dimensions={0} | all-to-all | bytes 3145728 | tf_op jit(solution)/shard_map/all_to_all | solution.py:107
  268.9 1.8 copy-done.3
  271.1 5.0 %maximum_add_fusion = f32[1,3072,2,1,128]{4,3,2,1,0:T(1,128)} fusion(f32[1,3072,2,1,128]{4,3,2,1,0:T(1,128)S(1)} %copy-done.3, f32[1,3072,1,1,128]{4,3,2,1,0:T(1,128)S(1)} %bitcast.526, f32[1,3072,1,1,128]{4,3,2,1,0:T(1,128)S(1)} %bitcast.523), kind=kLoop, calls=%fused_computation.40 | loop fusion | flops 1572864 | bytes 9437184 | tf_op jit(solution)/shard_map/add | solution.py:97
  276.1 29.5 %collective-permute-done = bf16[32,3,64,128]{3,2,1,0:T(8,128)(2,1)S(1)} collective-permute-done((bf16[32,3,64,128]{3,2,1,0:T(8,128)(2,1)S(1)}, bf16[32,3,64,128]{3,2,1,0:T(8,128)(2,1)S(1)}, u32[]{:S(2)}, u32[]{:S(2)}) %collective-permute-start) | collective-permute-done | bytes 1572896 | tf_op jit(solution)/shard_map/ppermute | solution.py:14
  305.8 2.1 reshape.136
  (151 shorter events, 24.5 us)
Async XLA Ops:
  0.6 14.0 %copy-start.7 = (bf16[1,32,3,8192]{3,1,2,0:T(8,128)(2,1)S(1)}, bf16[1,32,3,8192]{3,1,2,0:T(8,128)(2,1)}, u32[]{:S(2)}) copy-start(bf16[1,32,3,8192]{3,1,2,0:T(8,128)(2,1)} %param.8) | copy-start | bytes 4718596
  3.1 28.3 %all-to-all-start.1 = ((bf16[32,1,64,128]{3,0,1,2:T(8,128)(2,1)}), bf16[32,1,64,128]{3,0,1,2:T(8,128)(2,1)S(1)}, u32[]{:S(2)}, u32[]{:S(2)}) async-start(bf16[32,1,64,128]{3,0,1,2:T(8,128)(2,1)} %copy.303), calls=%async_computation.1 | async-start | bytes 1048576 | tf_op jit(solution)/shard_map/all_to_all | solution.py:28
  31.3 0.8 copy-start.4
  32.1 46.0 %all-to-all-start = ((bf16[32,3,64,128]{3,0,1,2:T(8,128)(2,1)}), bf16[32,3,64,128]{3,0,1,2:T(8,128)(2,1)}, u32[]{:S(2)}, u32[]{:S(2)}) async-start(bf16[32,3,64,128]{3,0,1,2:T(8,128)(2,1)} %copy.300), calls=%async_computation | async-start | bytes 3145728 | tf_op jit(solution)/shard_map/all_to_all | solution.py:27
  43.3 2.4 copy-start.5
  79.8 1.3 copy-start.2
  89.9 4.0 %copy-start = (f32[512,5120]{1,0:T(8,128)}, f32[512,5120]{1,0:T(8,128)S(1)}, u32[]{:S(2)}) copy-start(f32[512,5120]{1,0:T(8,128)S(1)} %get-tuple-element.320) | copy-start | bytes 31457284 | tf_op jit(solution)/shard_map/while
  93.9 1.6 copy-start.10
  95.5 7.9 %copy-start.1 = (f32[512,5120]{1,0:T(8,128)S(1)}, f32[512,5120]{1,0:T(8,128)}, u32[]{:S(2)}) copy-start(f32[512,5120]{1,0:T(8,128)} %copy-done) | copy-start | bytes 31457284 | tf_op jit(solution)/shard_map/while
  95.5 7.9 %copy-start.9 = (bf16[5120,1,128]{2,0,1:T(8,128)(2,1)S(1)}, bf16[5120,1,128]{2,0,1:T(8,128)(2,1)}, u32[]{:S(2)}) copy-start(bf16[5120,1,128]{2,0,1:T(8,128)(2,1)} %get-tuple-element.360) | copy-start | bytes 3932164 | tf_op jit(solution)/shard_map/while
  110.2 2.5 copy-start.8
  122.0 4.0 %copy-start = (f32[512,5120]{1,0:T(8,128)}, f32[512,5120]{1,0:T(8,128)S(1)}, u32[]{:S(2)}) copy-start(f32[512,5120]{1,0:T(8,128)S(1)} %get-tuple-element.320) | copy-start | bytes 31457284 | tf_op jit(solution)/shard_map/while
  126.0 1.6 copy-start.10
  127.6 8.7 %copy-start.1 = (f32[512,5120]{1,0:T(8,128)S(1)}, f32[512,5120]{1,0:T(8,128)}, u32[]{:S(2)}) copy-start(f32[512,5120]{1,0:T(8,128)} %copy-done) | copy-start | bytes 31457284 | tf_op jit(solution)/shard_map/while
  127.6 8.7 %copy-start.9 = (bf16[5120,1,128]{2,0,1:T(8,128)(2,1)S(1)}, bf16[5120,1,128]{2,0,1:T(8,128)(2,1)}, u32[]{:S(2)}) copy-start(bf16[5120,1,128]{2,0,1:T(8,128)(2,1)} %get-tuple-element.360) | copy-start | bytes 3932164 | tf_op jit(solution)/shard_map/while
  143.0 2.5 copy-start.8
  154.8 4.0 %copy-start = (f32[512,5120]{1,0:T(8,128)}, f32[512,5120]{1,0:T(8,128)S(1)}, u32[]{:S(2)}) copy-start(f32[512,5120]{1,0:T(8,128)S(1)} %get-tuple-element.320) | copy-start | bytes 31457284 | tf_op jit(solution)/shard_map/while
  158.8 1.6 copy-start.10
  160.4 8.7 %copy-start.1 = (f32[512,5120]{1,0:T(8,128)S(1)}, f32[512,5120]{1,0:T(8,128)}, u32[]{:S(2)}) copy-start(f32[512,5120]{1,0:T(8,128)} %copy-done) | copy-start | bytes 31457284 | tf_op jit(solution)/shard_map/while
  160.4 8.7 %copy-start.9 = (bf16[5120,1,128]{2,0,1:T(8,128)(2,1)S(1)}, bf16[5120,1,128]{2,0,1:T(8,128)(2,1)}, u32[]{:S(2)}) copy-start(bf16[5120,1,128]{2,0,1:T(8,128)(2,1)} %get-tuple-element.360) | copy-start | bytes 3932164 | tf_op jit(solution)/shard_map/while
  175.8 2.5 copy-start.8
  187.7 4.0 %copy-start = (f32[512,5120]{1,0:T(8,128)}, f32[512,5120]{1,0:T(8,128)S(1)}, u32[]{:S(2)}) copy-start(f32[512,5120]{1,0:T(8,128)S(1)} %get-tuple-element.320) | copy-start | bytes 31457284 | tf_op jit(solution)/shard_map/while
  191.6 1.6 copy-start.10
  193.2 8.7 %copy-start.1 = (f32[512,5120]{1,0:T(8,128)S(1)}, f32[512,5120]{1,0:T(8,128)}, u32[]{:S(2)}) copy-start(f32[512,5120]{1,0:T(8,128)} %copy-done) | copy-start | bytes 31457284 | tf_op jit(solution)/shard_map/while
  193.2 8.7 %copy-start.9 = (bf16[5120,1,128]{2,0,1:T(8,128)(2,1)S(1)}, bf16[5120,1,128]{2,0,1:T(8,128)(2,1)}, u32[]{:S(2)}) copy-start(bf16[5120,1,128]{2,0,1:T(8,128)(2,1)} %get-tuple-element.360) | copy-start | bytes 3932164 | tf_op jit(solution)/shard_map/while
  208.7 2.5 copy-start.8
  217.5 2.5 copy-start.6
  267.9 37.7 %collective-permute-start = (bf16[32,3,64,128]{3,2,1,0:T(8,128)(2,1)S(1)}, bf16[32,3,64,128]{3,2,1,0:T(8,128)(2,1)S(1)}, u32[]{:S(2)}, u32[]{:S(2)}) collective-permute-start(bf16[32,3,64,128]{3,2,1,0:T(8,128)(2,1)S(1)} %copy.372), channel_id=1, source_target_pairs={{64,0},{128,64},{192,128},{0,192},{65,1},{129,65},{193,129},{1,193... | collective-permute-start | bytes 4718600 | tf_op jit(solution)/shard_map/ppermute | solution.py:14
  268.8 1.9 copy-start.3
  268.8 2.4 slice-start
